TPU v7x, 32 devices: a whole 2x2x4 slice. The times are simulated.
32 devices in a mesh: groups: 2 (over x), wide: 16 (over z, y, core).
Axes of the slice: x: 2, y: 2, z: 4, core: 2. Of those that a mesh axis runs over, the one named last changes fastest.
Arguments:
- queries: bfloat16 [4096, 512], P(('groups', 'wide')), parts along dimension 0, may hold values from -200 to 200, as said below
- tree_kv: bfloat16 [2, 4096, 128], P(None, ('groups', 'wide')), parts along dimension 1, may hold values from -7 to 7, as said below
- kv_cache: bfloat16 [2, 512, 32, 128], P(None, ('groups', 'wide')), parts along dimension 1, may hold values from -6 to 6, as said below
- block_table: int32 [128, 4], P(('groups', 'wide')), parts along dimension 0, may hold values from 0 to 15, as said below
- cache_lengths: int32 [32, 4], P(('groups', 'wide')), parts along dimension 0, may hold values from 1 to 128, as said below
- parents: int32 [128, 32], P(('groups', 'wide')), parts along dimension 0, may hold values from -1 to 30, as said below
- w_out: bfloat16 [8192, 2048], P('wide'), may hold values from -0.375 to 0.375, as said below
- w_gate: bfloat16 [16, 2048, 768], P('wide'), may hold values from -0.125 to 0.125
- w_up: bfloat16 [16, 2048, 768], P('wide'), may hold values from -0.125 to 0.125
- w_down: bfloat16 [16, 768, 2048], P('wide'), may hold values from -0.4375 to 0.4375
- expert_ids: int32 [512, 8], P(('groups', 'wide')), parts along dimension 0, may hold values from 0 to 15, as said below
- gate_weights: float32 [512, 8], P(('groups', 'wide')), parts along dimension 0, may hold values from 0.05 to 0.5
Outputs:
- mixed: bfloat16 [512, 2048], P(('groups', 'wide')), parts along dimension 0
There are 2 independent parts, one for each index of `groups`. A program takes and returns all parts, laid end to end along the dimension named above; an argument that names none is the same for every part. Nothing has to cross between parts.
Inputs may be any that keep to these rules, and one draw needn't show every extreme that they name: `queries`: its hidden draw may carry large entries. `tree_kv`: blocks of one group whose slices use the same key head are equal. `kv_cache`: pools of one group whose slices use the same key head are equal. `block_table`: each device's rows list every page of its pool once; blocks t * 2 + g are equal for all t. `cache_lengths`: rows t * 2 + g are equal for all t; every row holds one length 128 and one length 1. `parents`: node i of a tree has a parent before it; node 0 is the root with parent -1; blocks t * 2 + g are equal for all t. `w_out`: blocks of one head slice are equal. `expert_ids`: each row lists 8 different experts. Within the rows of one device no expert is listed by more than 10 rows; in every draw one expert is listed by exactly 10 rows of every device.
All inputs are finite; a program needn't handle non-finite values.
Results may differ from a plain program's by a relative error of at most 0.0083.
Values may be sent and summed in bfloat16 or wider, within the bound.
A program may use at most 64 MiB of HBM per device.

v0:
```python
import jax
import jax.numpy as jnp
from jax import lax
from jax.sharding import PartitionSpec as P

ATT_TP = 8


def from_partner(block, axis, apart):
    count = lax.axis_size(axis)
    route = []
    for low in range(count):
        high = low | 1 << apart
        if high != low and high < count:
            route += [(low, high), (high, low)]
    return lax.ppermute(block, axis, route)


def ancestor_mask(parents):
    node_count = parents.shape[1]
    columns = jnp.arange(node_count, dtype=jnp.int32)
    linked = (parents[:, :, None] == columns).astype(jnp.float32) + jnp.eye(
        node_count, dtype=jnp.float32
    )
    for repeat in range(max(node_count - 1, 1).bit_length()):
        linked = jnp.minimum(
            jnp.einsum("sij,sjk->sik", linked, linked, precision=lax.Precision.HIGHEST), 1.0
        )
    return linked > 0.5


def attend_local(queries, tree_kv, kv_cache, block_table, cache_lengths, parents):
    seq_count = parents.shape[0]
    node_count = parents.shape[1]
    head_dim = tree_kv.shape[-1]
    head_count = queries.shape[1] // head_dim
    cached_rows = kv_cache[:, block_table].reshape(2, seq_count, -1, head_dim)
    cached = cached_rows.shape[2]
    own_tree = tree_kv.reshape(2, seq_count, node_count, head_dim)
    joined = jnp.concatenate([cached_rows, own_tree], axis=2)
    query_heads = queries.reshape(seq_count, node_count, head_count, head_dim)
    scores = jnp.einsum(
        "sqhd,skd->sqhk", query_heads, joined[0], preferred_element_type=jnp.float32
    ) * head_dim ** (-0.5)
    positions = jnp.arange(cached, dtype=jnp.int32)
    cache_open = jnp.broadcast_to(
        positions[None, None, :] < cache_lengths.reshape(seq_count, 1, 1),
        (seq_count, node_count, cached),
    )
    allowed = jnp.concatenate([cache_open, ancestor_mask(parents)], axis=2)[:, :, None, :]
    masked = jnp.where(allowed, scores, -jnp.inf)
    highest = jnp.max(masked, axis=-1, keepdims=True)
    weights = jnp.exp(masked - highest)
    denominator = jnp.sum(weights, axis=-1, keepdims=True)
    blended = jnp.einsum(
        "sqhk,skd->sqhd",
        weights.astype(jnp.bfloat16),
        joined[1],
        preferred_element_type=jnp.float32,
    )
    return (blended / denominator).reshape(seq_count * node_count, -1).astype(jnp.bfloat16)


def expert_rows(received, w_gate, w_up, w_down):
    feature_count = received.shape[-1]
    flattened = received.reshape(-1, feature_count)
    gate_part = jnp.dot(flattened, w_gate[0], preferred_element_type=jnp.float32)
    up_part = jnp.dot(flattened, w_up[0], preferred_element_type=jnp.float32)
    activated = (jax.nn.silu(gate_part) * up_part).astype(jnp.bfloat16)
    produced = jnp.dot(activated, w_down[0], preferred_element_type=jnp.float32).astype(
        jnp.bfloat16
    )
    return produced.reshape(received.shape)


def body(
    queries,
    tree_kv,
    kv_cache,
    block_table,
    cache_lengths,
    parents,
    w_out,
    w_gate,
    w_up,
    w_down,
    expert_ids,
    gate_weights,
):
    attended = attend_local(queries, tree_kv, kv_cache, block_table, cache_lengths, parents)
    projected = jnp.dot(attended, w_out, preferred_element_type=jnp.float32)
    axis_width = lax.axis_size("wide")
    device_index = lax.axis_index("wide")
    top_bit = axis_width.bit_length() - 1
    slice_bits = [top_bit - 1 - step for step in range(ATT_TP.bit_length() - 1)]
    buffer = projected
    for bit in slice_bits:
        half_rows = buffer.shape[0] // 2
        upper_bit = device_index // (1 << bit) % 2 == 1
        kept_half = jnp.where(upper_bit, buffer[half_rows:], buffer[:half_rows])
        sent_half = jnp.where(upper_bit, buffer[:half_rows], buffer[half_rows:])
        buffer = kept_half + from_partner(sent_half, "wide", bit)
    hidden = buffer.astype(jnp.bfloat16)
    row_count = hidden.shape[0]
    mean_rows = row_count * expert_ids.shape[1] // axis_width
    capacity = mean_rows + max(mean_rows // 4, 1)
    numbers = jnp.arange(axis_width, dtype=jnp.int32)
    matches = expert_ids[:, :, None] == numbers
    chosen = jnp.any(matches, axis=1).astype(jnp.int32)
    row_weight = jnp.sum(jnp.where(matches, gate_weights[:, :, None], 0.0), axis=1)
    ranking = jnp.cumsum(chosen, axis=0) - chosen
    slot_ids = jnp.arange(capacity, dtype=jnp.int32)
    placed = (chosen[:, :, None] == 1) & (ranking[:, :, None] == slot_ids)
    placed_int = placed.astype(jnp.int32)
    source_row = jnp.sum(placed_int * jnp.arange(row_count, dtype=jnp.int32)[:, None, None], axis=0)
    occupied = jnp.sum(placed_int, axis=0)
    slot_weight = jnp.sum(jnp.where(placed, row_weight[:, :, None], 0.0), axis=0)
    outgoing = jnp.where(occupied[:, :, None] == 1, hidden[source_row], jnp.zeros((), jnp.bfloat16))
    received = lax.all_to_all(outgoing, "wide", split_axis=0, concat_axis=0, tiled=True)
    returned = lax.all_to_all(
        expert_rows(received, w_gate, w_up, w_down), "wide", split_axis=0, concat_axis=0, tiled=True
    )
    weighted = returned.reshape(-1, returned.shape[-1]).astype(jnp.float32) * slot_weight.reshape(
        -1, 1
    )
    combined = jax.ops.segment_sum(weighted, source_row.reshape(-1), num_segments=row_count)
    return combined.astype(jnp.bfloat16)


def solution(mesh):
    placed = (
        P(("groups", "wide"), None),
        P(None, ("groups", "wide"), None),
        P(None, ("groups", "wide"), None, None),
        P(("groups", "wide"), None),
        P(("groups", "wide"), None),
        P(("groups", "wide"), None),
        P("wide", None),
        P("wide", None, None),
        P("wide", None, None),
        P("wide", None, None),
        P(("groups", "wide"), None),
        P(("groups", "wide"), None),
    )
    return jax.shard_map(
        body, mesh=mesh, in_specs=placed, out_specs=P(("groups", "wide"), None), check_vma=False
    )
```

profile of v0, /device:TPU:0, one launch (start us, length us, event | category | flops | bytes accessed | tf_op | source)
XLA Modules:
  0.0 141.4 jit_solution(13651653561778178837)
XLA Ops:
  0.0 1.5 %iota_compare_fusion.5 = pred[4,128]{1,0:T(4,128)(4,1)} fusion(s32[4]{0:T(128)} %bitcast.67), kind=kLoop, calls=%fused_computation.78 | loop fusion | flops 512 | bytes 528 | tf_op jit(solution)/shard_map/lt | solution.py:47
  1.5 0.7 compare_select_fusion.1
  2.2 0.1 reshape.103
  2.2 0.6 pad_clamp_fusion.1
  2.8 1.0 convolution_minimum_fusion.4
  3.9 0.2 convolution_minimum_fusion.3
  4.1 0.2 convolution_minimum_fusion.2
  4.3 0.2 convolution_minimum_fusion.1
  4.5 0.2 fusion.20
  4.7 0.9 reshape.97
  5.6 1.7 %gather_fusion = bf16[16,2,32,128]{3,2,1,0:T(8,128)(2,1)S(1)} fusion(bf16[2,16,32,128]{3,2,1,0:T(8,128)(2,1)} %param.14, s32[1024]{0:T(1024)} %pad_clamp_fusion.1), kind=kCustom, calls=%fused_computation | custom fusion | bytes 524352 | tf_op jit(solution)/shard_map/gather | solution.py:37
  7.3 0.8 broadcast_in_dim.78
  8.2 1.1 fusion.55
  9.3 0.3 fusion.29
  9.6 0.3 fusion.19
  10.0 0.4 fusion.40
  10.4 1.0 copy-done.1
  11.4 0.9 slice_select_fusion
  12.3 4.1 %collective-permute-start = (f32[64,2048]{1,0:T(8,128)}, f32[64,2048]{1,0:T(8,128)}, u32[]{:S(2)}, u32[]{:S(2)}) collective-permute-start(f32[64,2048]{1,0:T(8,128)} %slice_select_fusion), channel_id=1, source_target_pairs={{0,8},{8,0},{1,9},{9,1},{2,10},{10,2},{3,11},{11,3},{4,12},{12,4},... | collective-permute-start | bytes 1572872 | tf_op jit(solution)/shard_map/ppermute | solution.py:16
  16.5 0.1 fusion.47
  16.6 23.2 %collective-permute-done = f32[64,2048]{1,0:T(8,128)} collective-permute-done((f32[64,2048]{1,0:T(8,128)}, f32[64,2048]{1,0:T(8,128)}, u32[]{:S(2)}, u32[]{:S(2)}) %collective-permute-start) | collective-permute-done | bytes 524320 | tf_op jit(solution)/shard_map/ppermute | solution.py:16
  39.9 1.4 %select_add_fusion = f32[64,2048]{1,0:T(8,128)S(1)} fusion(f32[64,2048]{1,0:T(8,128)} %collective-permute-done, f32[128,2048]{1,0:T(8,128)} %copy-done.1, pred[]{:T(512)S(6)} %eq.93), kind=kLoop, calls=%fused_computation.27 | loop fusion | flops 262144 | bytes 2097153 | tf_op jit(solution)/shard_map/add | solution.py:102
  41.3 0.8 copy-done.2
  42.1 0.8 collective-permute-start.1
  43.0 6.8 %collective-permute-done.1 = f32[32,2048]{1,0:T(8,128)} collective-permute-done((f32[32,2048]{1,0:T(8,128)S(1)}, f32[32,2048]{1,0:T(8,128)}, u32[]{:S(2)}, u32[]{:S(2)}) %collective-permute-start.1) | collective-permute-done | bytes 262176 | tf_op jit(solution)/shard_map/ppermute | solution.py:16
  49.8 1.1 select_add_fusion.1
  50.9 0.7 slice_select_fusion.2
  51.6 1.3 collective-permute-start.2
  52.9 0.1 copy.31
  53.1 0.1 reshape.111
  53.2 3.7 %collective-permute-done.2 = f32[16,2048]{1,0:T(8,128)} collective-permute-done((f32[16,2048]{1,0:T(8,128)}, f32[16,2048]{1,0:T(8,128)}, u32[]{:S(2)}, u32[]{:S(2)}) %collective-permute-start.2) | collective-permute-done | bytes 131104 | tf_op jit(solution)/shard_map/ppermute | solution.py:16
  56.8 0.9 add_convert_fusion
  57.8 1.9 %gather_fusion.1 = bf16[160,2048]{1,0:T(8,128)(2,1)} fusion(bf16[16,2048]{1,0:T(8,128)(2,1)S(1)} %add_convert_fusion, s32[1024]{0:T(1024)S(1)} %pad_clamp_fusion), kind=kCustom, calls=%fused_computation.1 | custom fusion | bytes 1311360 | tf_op jit(solution)/shard_map/gather | solution.py:118
  59.7 2.2 %reshape.110 = bf16[16,10,2048]{2,1,0:T(8,128)(2,1)} reshape(bf16[160,2048]{1,0:T(8,128)(2,1)} %gather_fusion.1) | data formatting | bytes 1310720 | tf_op jit(solution)/shard_map/gather | solution.py:118
  61.9 1.4 broadcast_select_fusion
  63.2 31.2 %all_to_all.10 = bf16[16,10,2048]{2,1,0:T(8,128)(2,1)} all-to-all(bf16[16,10,2048]{2,1,0:T(8,128)(2,1)S(1)} %broadcast_select_fusion), channel_id=1, replica_groups=mesh['groups'=2,'wide'=16] {'wide'}, dimensions={0} | all-to-all | bytes 1310720 | tf_op jit(solution)/shard_map/all_to_all | solution.py:119
  94.4 2.2 %reshape.98 = bf16[160,2048]{1,0:T(8,128)(2,1)} reshape(bf16[16,10,2048]{2,1,0:T(8,128)(2,1)} %all_to_all.10) | data formatting | bytes 1310720 | tf_op jit(solution)/shard_map/reshape | solution.py:66
  96.6 3.6 %fusion.4 = f32[160,768]{1,0:T(8,128)} fusion(bf16[160,2048]{1,0:T(8,128)(2,1)} %reshape.98, bf16[1,2048,768]{2,1,0:T(8,128)(2,1)} %param.19), kind=kOutput, calls=%fused_computation.7 | convolution fusion | flops 503316480 | bytes 4292608 | tf_op jit(solution)/shard_map/dot_general | solution.py:67
  100.2 4.5 %fusion.6 = bf16[160,2048]{1,0:T(8,128)(2,1)} fusion(bf16[1,768,2048]{2,1,0:T(8,128)(2,1)S(1)} %copy-done, bf16[160,2048]{1,0:T(8,128)(2,1)} %reshape.98, bf16[1,2048,768]{2,1,0:T(8,128)(2,1)} %param.20, f32[160,768]{1,0:T(8,128)} %fusion.4), kind=kOutput, calls=%fused_computation.9 | convolution fusion | flops 1007697920 | bytes 8093696 | tf_op jit(solution)/shard_map/dot_general | solution.py:70
  104.6 2.2 %reshape.99 = bf16[16,10,2048]{2,1,0:T(8,128)(2,1)} reshape(bf16[160,2048]{1,0:T(8,128)(2,1)} %fusion.6) | data formatting | bytes 1310720 | tf_op jit(solution)/shard_map/reshape | solution.py:73
  106.8 5.1 %all-to-all-start.1 = ((bf16[16,10,2048]{2,1,0:T(8,128)(2,1)}), bf16[16,10,2048]{2,1,0:T(8,128)(2,1)}, u32[]{:S(2)}, u32[]{:S(2)}) async-start(bf16[16,10,2048]{2,1,0:T(8,128)(2,1)} %reshape.99), calls=%async_computation.1 | async-start | bytes 2097152 | tf_op jit(solution)/shard_map/all_to_all | solution.py:120
  112.1 0.1 select_reduce_fusion.2
  112.3 0.1 mul.41
  112.4 0.1 reshape.119
  112.5 22.4 %all-to-all-done.1 = bf16[16,10,2048]{2,1,0:T(8,128)(2,1)} async-done(((bf16[16,10,2048]{2,1,0:T(8,128)(2,1)}), bf16[16,10,2048]{2,1,0:T(8,128)(2,1)}, u32[]{:S(2)}, u32[]{:S(2)}) %all-to-all-start.1) | async-done | bytes 655392 | tf_op jit(solution)/shard_map/all_to_all | solution.py:120
  134.9 2.4 %reshape.100 = f32[160,2048]{1,0:T(8,128)} reshape(bf16[16,10,2048]{2,1,0:T(8,128)(2,1)} %all-to-all-done.1) | data formatting | bytes 1966080 | tf_op jit(solution)/shard_map/convert_element_type | solution.py:123
  137.2 3.5 %scatter_custom_fusion = f32[16,2048]{1,0:T(8,128)S(1)} fusion(s32[160]{0:T(256)S(1)} %reshape.119, f32[160,2048]{1,0:T(8,128)} %reshape.100, f32[160]{0:T(256)S(1)} %mul.41, f32[]{:T(128)} %constant.71.clone.1), kind=kCustom, calls=%fused_computation.10 | custom fusion | flops 655360 | bytes 1442820 | tf_op jit(solution)/shard_map/scatter-add | solution.py:126
  140.7 0.6 convert_element_type.66
  (30 shorter events, 0.7 us)
Async XLA Ops:
  0.0 100.2 %copy-start = (bf16[1,768,2048]{2,1,0:T(8,128)(2,1)S(1)}, bf16[1,768,2048]{2,1,0:T(8,128)(2,1)}, u32[]{:S(2)}) copy-start(bf16[1,768,2048]{2,1,0:T(8,128)(2,1)} %param.21) | copy-start | bytes 9437188
  7.3 2.3 %copy-start.6 = (bf16[2,128,128]{2,1,0:T(8,128)(2,1)S(1)}, bf16[2,128,128]{2,1,0:T(8,128)(2,1)}, u32[]{:S(2)}) copy-start(bf16[2,128,128]{2,1,0:T(8,128)(2,1)} %param.13) | copy-start | bytes 196612
  7.3 2.7 %copy-start.3 = (bf16[512,2048]{1,0:T(8,128)(2,1)S(1)}, bf16[512,2048]{1,0:T(8,128)(2,1)}, u32[]{:S(2)}) copy-start(bf16[512,2048]{1,0:T(8,128)(2,1)} %param.18) | copy-start | bytes 6291460
  10.0 6.4 %copy-start.4 = (s32[16,8]{0,1:T(8,128)S(1)}, s32[16,8]{0,1:T(8,128)}, u32[]{:S(2)}) copy-start(s32[16,8]{0,1:T(8,128)} %param.22) | copy-start | bytes 1540
  10.4 1.0 copy-start.1
  12.3 27.6 %collective-permute-start = (f32[64,2048]{1,0:T(8,128)}, f32[64,2048]{1,0:T(8,128)}, u32[]{:S(2)}, u32[]{:S(2)}) collective-permute-start(f32[64,2048]{1,0:T(8,128)} %slice_select_fusion), channel_id=1, source_target_pairs={{0,8},{8,0},{1,9},{9,1},{2,10},{10,2},{3,11},{11,3},{4,12},{12,4},... | collective-permute-start | bytes 1572872 | tf_op jit(solution)/shard_map/ppermute | solution.py:16
  41.3 0.8 copy-start.2
  42.1 7.6 %collective-permute-start.1 = (f32[32,2048]{1,0:T(8,128)S(1)}, f32[32,2048]{1,0:T(8,128)}, u32[]{:S(2)}, u32[]{:S(2)}) collective-permute-start(f32[32,2048]{1,0:T(8,128)S(1)} %slice_select_fusion.1), channel_id=1, source_target_pairs={{0,4},{4,0},{1,5},{5,1},{2,6},{6,2},{3,7},{7,3},{8,12},{12,8},{9,1... | collective-permute-start | bytes 786440 | tf_op jit(solution)/shard_map/ppermute | solution.py:16
  51.6 5.3 %collective-permute-start.2 = (f32[16,2048]{1,0:T(8,128)}, f32[16,2048]{1,0:T(8,128)}, u32[]{:S(2)}, u32[]{:S(2)}) collective-permute-start(f32[16,2048]{1,0:T(8,128)} %slice_select_fusion.2), channel_id=1, source_target_pairs={{0,2},{2,0},{1,3},{3,1},{4,6},{6,4},{5,7},{7,5},{8,10},{10,8},{9,1... | collective-permute-start | bytes 393224 | tf_op jit(solution)/shard_map/ppermute | solution.py:16
  104.6 7.4 %copy-start.5 = (f32[16,8]{0,1:T(8,128)S(1)}, f32[16,8]{0,1:T(8,128)}, u32[]{:S(2)}) copy-start(f32[16,8]{0,1:T(8,128)} %param.23) | copy-start | bytes 1540
  106.8 28.0 %all-to-all-start.1 = ((bf16[16,10,2048]{2,1,0:T(8,128)(2,1)}), bf16[16,10,2048]{2,1,0:T(8,128)(2,1)}, u32[]{:S(2)}, u32[]{:S(2)}) async-start(bf16[16,10,2048]{2,1,0:T(8,128)(2,1)} %reshape.99), calls=%async_computation.1 | async-start | bytes 2097152 | tf_op jit(solution)/shard_map/all_to_all | solution.py:120
where the time goes:
time: 143 us; the launch traced here: 141 us
  waiting for transfers between devices  56 us (39%)
  blocking collectives  31.2 us (22%)
  local copies, waits for them, and re-layouts  17 us (12%)
  other arithmetic  14 us (10%)
  matrix products  11.6 us (8%)
  starting transfers between devices  11.3 us (8%)
    ppermute x3, waiting for transfers between devices, from_partner(): return lax.ppermute(block, axis, route)  33.7 us
    all_to_all x1, blocking collectives, body(): lax.all_to_all(outgoing, 'wide', split_axis=0, concat_axis=0, tiled=True)  31.2 us
    all_to_all x1, waiting for transfers between devices, body(): lax.all_to_all(expert_rows(received, w_gate, w_up, w_down), 'wide', split...  22.4 us
    ppermute x3, starting transfers between devices, from_partner(): return lax.ppermute(block, axis, route)  6.19 us
    all_to_all x1, starting transfers between devices, body(): lax.all_to_all(expert_rows(received, w_gate, w_up, w_down), 'wide', split...  5.08 us
    dot_general x1, matrix products, expert_rows(): jnp.dot(activated, w_down[0], preferred_element_type=jnp.float32)  4.47 us
    gather x2, local copies, waits for them, and re-layouts, body(): hidden[source_row]  4.08 us
    dot_general x1, matrix products, expert_rows(): jnp.dot(flattened, w_gate[0], preferred_element_type=jnp.float32)  3.55 us
  transfers between devices with their start and end apart: 4, of which 4 were waited for; matrix products, arithmetic and copies ran while one was open for 1% of the time, Pallas kernels for 0%

commit v1 on v0

v1 whole, which is shorter than its diff:
```python
import functools

import jax
import jax.numpy as jnp
from jax import lax
from jax.experimental import pallas as pl
from jax.experimental.pallas import tpu as pltpu
from jax.sharding import PartitionSpec as P

ATT_TP = 8
CHUNKS = 4
TILE = 256
LANES = 128
MESH = pl.DeviceIdType.MESH


def spread(bits):
    offsets = [0]
    for bit in bits:
        offsets += [offset + (1 << bit) for offset in offsets]
    return offsets


def swapped(bits, low):
    other = list(bits)
    if len(other) > low + 1:
        other[low], other[low + 1] = other[low + 1], other[low]
    return other


def layer_kernel(
    count,
    block_table,
    cache_lengths,
    queries_in,
    tree_in,
    cache_in,
    parents,
    w_out_in,
    w_gate_in,
    w_up_in,
    w_down_in,
    expert_ids,
    gate_weights,
    out,
    queries,
    tree,
    cache,
    w_out,
    w_gate,
    w_up,
    w_down,
    attended,
    partial,
    hidden,
    routing,
    gate_sum,
    up_sum,
    activated,
    produced,
    send_one,
    recv_one,
    send_two,
    recv_two,
    load_sem,
    one_send_sem,
    one_recv_sem,
    all_send_sem,
    all_recv_sem,
    route_send_sem,
    route_recv_sem,
    two_send_sem,
    two_recv_sem,
):
    me = lax.axis_index("wide")
    bit_count = count.bit_length() - 1
    slice_shift = bit_count - (ATT_TP.bit_length() - 1)
    mine = [(me // (1 << bit)) % 2 for bit in range(bit_count)]
    partner = [me + (1 - 2 * mine[bit]) * (1 << bit) for bit in range(bit_count)]

    barrier = pltpu.get_barrier_semaphore()
    for bit in range(bit_count):
        pl.semaphore_signal(
            barrier, inc=1, device_id={"wide": partner[bit]}, device_id_type=MESH
        )

    loads = []
    for number, (source, target) in enumerate(
        (
            (queries_in, queries),
            (tree_in, tree),
            (cache_in, cache),
            (w_out_in, w_out),
            (w_gate_in.at[0], w_gate),
            (w_up_in.at[0], w_up),
            (w_down_in.at[0], w_down),
        )
    ):
        copy = pltpu.make_async_copy(source, target, load_sem.at[number])
        copy.start()
        loads.append(copy)

    rows = out.shape[0]
    lane_ids = lax.broadcasted_iota(jnp.int32, (rows, routing.shape[2]), 1)
    row_weight = jnp.zeros((rows, routing.shape[2]), jnp.float32)
    for k in range(expert_ids.shape[1]):
        row_weight += jnp.where(
            expert_ids[:, k : k + 1] == lane_ids, gate_weights[:, k : k + 1], 0.0
        )
    routing[me] = row_weight

    seq_count, node_count = parents.shape
    head_dim = tree.shape[2]
    head_count = queries.shape[1] // head_dim
    page_count = block_table.shape[1]
    node_rows = lax.broadcasted_iota(jnp.int32, (node_count, node_count), 0)
    node_cols = lax.broadcasted_iota(jnp.int32, (node_count, node_count), 1)
    closures = []
    for seq in range(seq_count):
        linked = ((parents[seq : seq + 1, :] == node_rows) | (node_rows == node_cols)).astype(
            jnp.float32
        )
        closures.append(linked)
    for repeat in range(max(node_count - 1, 1).bit_length()):
        narrow = [linked.astype(jnp.bfloat16) for linked in closures]
        closures = [
            jnp.minimum(jnp.dot(linked, linked, preferred_element_type=jnp.float32), 1.0)
            for linked in narrow
        ]

    for copy in loads[:3]:
        copy.wait()
    cached = page_count * cache.shape[2]
    positions = lax.broadcasted_iota(jnp.int32, (head_count * node_count, cached), 1)
    across = (((1,), (1,)), ((), ()))
    for seq in range(seq_count):
        first = seq * node_count
        last = first + node_count
        stacked = jnp.concatenate(
            [
                queries[first:last, head * head_dim : (head + 1) * head_dim]
                for head in range(head_count)
            ],
            axis=0,
        )
        pages = [block_table[seq, page] for page in range(page_count)]
        keys = jnp.concatenate([cache[0, page] for page in pages], axis=0)
        values = jnp.concatenate([cache[1, page] for page in pages], axis=0)
        scale = head_dim ** (-0.5)
        cache_scores = (
            lax.dot_general(stacked, keys, across, preferred_element_type=jnp.float32) * scale
        )
        tree_scores = (
            lax.dot_general(
                stacked, tree[0, first:last], across, preferred_element_type=jnp.float32
            )
            * scale
        )
        seen = jnp.concatenate([closures[seq].T] * head_count, axis=0) > 0.5
        cache_scores = jnp.where(positions < cache_lengths[0, seq], cache_scores, -jnp.inf)
        tree_scores = jnp.where(seen, tree_scores, -jnp.inf)
        highest = jnp.maximum(
            jnp.max(cache_scores, axis=1, keepdims=True),
            jnp.max(tree_scores, axis=1, keepdims=True),
        )
        cache_probs = jnp.exp(cache_scores - highest)
        tree_probs = jnp.exp(tree_scores - highest)
        denominator = jnp.sum(cache_probs, axis=1, keepdims=True) + jnp.sum(
            tree_probs, axis=1, keepdims=True
        )
        blended = jnp.dot(
            cache_probs.astype(jnp.bfloat16), values, preferred_element_type=jnp.float32
        ) + jnp.dot(
            tree_probs.astype(jnp.bfloat16),
            tree[1, first:last],
            preferred_element_type=jnp.float32,
        )
        blended = (blended / denominator).astype(jnp.bfloat16)
        for head in range(head_count):
            attended[first:last, head * head_dim : (head + 1) * head_dim] = blended[
                head * node_count : (head + 1) * node_count
            ]

    started = []

    def send(source, target, send_sem, recv_sem, bit):
        copy = pltpu.make_async_remote_copy(
            src_ref=source,
            dst_ref=target,
            send_sem=send_sem,
            recv_sem=recv_sem,
            device_id={"wide": partner[bit]},
            device_id_type=MESH,
        )
        copy.start()
        started.append(copy)
        return copy

    width = w_out.shape[1] // CHUNKS
    spans = [slice(chunk * width, (chunk + 1) * width) for chunk in range(CHUNKS)]

    class Halving:
        def __init__(self, total, out_buffer, in_buffer, send_sems, recv_sems, shift, orders):
            self.total = total
            self.out_buffer = out_buffer
            self.in_buffer = in_buffer
            self.send_sems = send_sems
            self.recv_sems = recv_sems
            self.shift = shift
            self.orders = orders
            self.steps = len(orders[0])
            self.copies = {}

        def places(self, chunk, step):
            order = self.orders[chunk % 2]
            base = 0
            for bit in order[:step]:
                base = base + mine[bit] * (1 << (bit - self.shift))
            bit = order[step]
            offsets = spread([other - self.shift for other in order[step + 1 :]])
            weight = 1 << (bit - self.shift)
            kept = [base + mine[bit] * weight + offset for offset in offsets]
            sent = [base + (1 - mine[bit]) * weight + offset for offset in offsets]
            first = sum(1 << (self.steps - 1 - past) for past in range(step))
            return bit, kept, sent, first

        def start(self, chunk, step):
            bit, kept, sent, first = self.places(chunk, step)
            for number, place in enumerate(sent):
                self.out_buffer[chunk, first + number] = self.total[
                    place, :, spans[chunk]
                ].astype(jnp.bfloat16)
            region = pl.ds(first, len(sent))
            self.copies[chunk, step] = send(
                self.out_buffer.at[chunk, region],
                self.in_buffer.at[chunk, region],
                self.send_sems.at[chunk, step],
                self.recv_sems.at[chunk, step],
                bit,
            )

        def finish(self, chunk, step):
            bit, kept, sent, first = self.places(chunk, step)
            self.copies[chunk, step].wait_recv()
            for number, place in enumerate(kept):
                self.total[place, :, spans[chunk]] += self.in_buffer[
                    chunk, first + number
                ].astype(jnp.float32)

    class Doubling:
        def __init__(self, buffer, columns, send_sems, recv_sems, row, order):
            self.buffer = buffer
            self.columns = columns
            self.send_sems = send_sems
            self.recv_sems = recv_sems
            self.row = row
            self.order = order
            self.copies = {}

        def start(self, step):
            bit = self.order[step]
            offsets = [0]
            held = [me]
            for past in self.order[:step]:
                held += [place + (1 - 2 * mine[past]) * (1 << past) for place in held]
            for number, place in enumerate(held):
                view = self.buffer.at[place, :, self.columns]
                slot = (1 << step) - 1 + number
                self.copies[step, number] = send(
                    view, view, self.send_sems.at[self.row, slot],
                    self.recv_sems.at[self.row, slot], bit,
                )

        def finish(self, step):
            for number in range(1 << step):
                self.copies[step, number].wait_recv()

    all_bits = list(range(bit_count))
    slice_bits = all_bits[slice_shift:]
    first_sum = Halving(
        partial, send_one, recv_one, one_send_sem, one_recv_sem, slice_shift,
        (slice_bits, swapped(slice_bits, 0)),
    )
    second_orders = (all_bits, swapped(all_bits, 1))
    second_sum = Halving(
        produced, send_two, recv_two, two_send_sem, two_recv_sem, 0, second_orders
    )
    gathers = [
        Doubling(
            hidden, spans[chunk], all_send_sem, all_recv_sem, chunk, second_orders[chunk % 2][::-1]
        )
        for chunk in range(CHUNKS)
    ]
    route = Doubling(routing, slice(None), route_send_sem, route_recv_sem, 0, all_bits[::-1])

    loads[3].wait()
    pl.semaphore_wait(barrier, bit_count)
    for chunk in range(CHUNKS):
        projected = jnp.dot(
            attended[...], w_out[:, spans[chunk]], preferred_element_type=jnp.float32
        )
        partial[:, :, spans[chunk]] = projected.reshape(partial.shape[0], rows, width)
        first_sum.start(chunk, 0)
    route.start(0)
    for step in range(first_sum.steps):
        for chunk in range(CHUNKS):
            first_sum.finish(chunk, step)
            if step + 1 < first_sum.steps:
                first_sum.start(chunk, step + 1)
            else:
                hidden[me, :, spans[chunk]] = partial[
                    me // (1 << slice_shift), :, spans[chunk]
                ].astype(jnp.bfloat16)
                gathers[chunk].start(0)
    for step in range(bit_count):
        for chunk in range(CHUNKS):
            if step + 1 < bit_count:
                gathers[chunk].finish(step)
                gathers[chunk].start(step + 1)
        route.finish(step)
        if step + 1 < bit_count:
            route.start(step + 1)
    loads[4].wait()
    loads[5].wait()

    blocks = TILE // rows if count * rows > TILE else count
    groups = count // blocks
    tile_rows = blocks * rows
    hidden_width = w_gate.shape[1]
    cuts = [
        slice(start, min(start + TILE, hidden_width)) for start in range(0, hidden_width, TILE)
    ]

    def over_groups(step):
        if groups == 1:
            step(0)
        else:
            pl.loop(0, groups)(step)

    for chunk in range(CHUNKS):
        gathers[chunk].finish(bit_count - 1)

        def accumulate(group, chunk=chunk):
            taken = hidden[pl.ds(group * blocks, blocks), :, spans[chunk]].reshape(
                tile_rows, width
            )
            for cut in cuts:
                for sums, weights in ((gate_sum, w_gate), (up_sum, w_up)):
                    part = jnp.dot(
                        taken, weights[spans[chunk], cut], preferred_element_type=jnp.float32
                    )
                    if chunk == 0:
                        sums[group, :, cut] = part
                    else:
                        sums[group, :, cut] += part

        over_groups(accumulate)

    def activate(group):
        for cut in cuts:
            gate = gate_sum[group, :, cut]
            activated[group, :, cut] = (
                gate / (1.0 + jnp.exp(-gate)) * up_sum[group, :, cut]
            ).astype(jnp.bfloat16)

    over_groups(activate)
    loads[6].wait()
    for chunk in range(CHUNKS):

        def down(group, chunk=chunk):
            made = jnp.dot(
                activated[group], w_down[:, spans[chunk]], preferred_element_type=jnp.float32
            )
            table = routing[pl.ds(group * blocks, blocks)].reshape(tile_rows, routing.shape[2])
            experts = lax.broadcasted_iota(jnp.int32, table.shape, 1)
            weight = jnp.sum(jnp.where(experts == me, table, 0.0), axis=1, keepdims=True)
            produced[pl.ds(group * blocks, blocks), :, spans[chunk]] = (made * weight).reshape(
                blocks, rows, width
            )

        over_groups(down)
        second_sum.start(chunk, 0)
    for step in range(second_sum.steps):
        for chunk in range(CHUNKS):
            second_sum.finish(chunk, step)
            if step + 1 < second_sum.steps:
                second_sum.start(chunk, step + 1)
            else:
                out[:, spans[chunk]] = produced[me, :, spans[chunk]].astype(jnp.bfloat16)
    for copy in started:
        copy.wait_send()


def body(
    queries,
    tree_kv,
    kv_cache,
    block_table,
    cache_lengths,
    parents,
    w_out,
    w_gate,
    w_up,
    w_down,
    expert_ids,
    gate_weights,
):
    count = lax.axis_size("wide")
    rows = expert_ids.shape[0]
    features = w_out.shape[1]
    hidden_width = w_gate.shape[2]
    bit_count = count.bit_length() - 1
    slice_steps = ATT_TP.bit_length() - 1
    width = features // CHUNKS
    lanes = -(-count // LANES) * LANES
    blocks = TILE // rows if count * rows > TILE else count
    groups = count // blocks
    tile_rows = blocks * rows
    hbm = pl.BlockSpec(memory_space=pl.ANY)
    vmem = pl.BlockSpec(memory_space=pltpu.VMEM)
    smem = pl.BlockSpec(memory_space=pltpu.SMEM)
    dma = pltpu.SemaphoreType.DMA
    return pl.pallas_call(
        functools.partial(layer_kernel, count),
        out_shape=jax.ShapeDtypeStruct((rows, features), jnp.bfloat16),
        in_specs=[smem, smem, hbm, hbm, hbm, vmem, hbm, hbm, hbm, hbm, vmem, vmem],
        out_specs=vmem,
        scratch_shapes=[
            pltpu.VMEM(queries.shape, queries.dtype),
            pltpu.VMEM(tree_kv.shape, tree_kv.dtype),
            pltpu.VMEM(kv_cache.shape, kv_cache.dtype),
            pltpu.VMEM(w_out.shape, w_out.dtype),
            pltpu.VMEM(w_gate.shape[1:], w_gate.dtype),
            pltpu.VMEM(w_up.shape[1:], w_up.dtype),
            pltpu.VMEM(w_down.shape[1:], w_down.dtype),
            pltpu.VMEM(queries.shape, jnp.bfloat16),
            pltpu.VMEM((ATT_TP, rows, features), jnp.float32),
            pltpu.VMEM((count, rows, features), jnp.bfloat16),
            pltpu.VMEM((count, rows, lanes), jnp.float32),
            pltpu.VMEM((groups, tile_rows, hidden_width), jnp.float32),
            pltpu.VMEM((groups, tile_rows, hidden_width), jnp.float32),
            pltpu.VMEM((groups, tile_rows, hidden_width), jnp.bfloat16),
            pltpu.VMEM((count, rows, features), jnp.float32),
            pltpu.VMEM((CHUNKS, ATT_TP - 1, rows, width), jnp.bfloat16),
            pltpu.VMEM((CHUNKS, ATT_TP - 1, rows, width), jnp.bfloat16),
            pltpu.VMEM((CHUNKS, count - 1, rows, width), jnp.bfloat16),
            pltpu.VMEM((CHUNKS, count - 1, rows, width), jnp.bfloat16),
            dma((7,)),
            dma((CHUNKS, slice_steps)),
            dma((CHUNKS, slice_steps)),
            dma((CHUNKS, count - 1)),
            dma((CHUNKS, count - 1)),
            dma((1, count - 1)),
            dma((1, count - 1)),
            dma((CHUNKS, bit_count)),
            dma((CHUNKS, bit_count)),
        ],
        compiler_params=pltpu.CompilerParams(
            collective_id=0, has_side_effects=True, vmem_limit_bytes=60 << 20
        ),
    )(
        block_table,
        cache_lengths,
        queries,
        tree_kv,
        kv_cache,
        parents,
        w_out,
        w_gate,
        w_up,
        w_down,
        expert_ids,
        gate_weights,
    )


def solution(mesh):
    placed = (
        P(("groups", "wide"), None),
        P(None, ("groups", "wide"), None),
        P(None, ("groups", "wide"), None, None),
        P(("groups", "wide"), None),
        P(("groups", "wide"), None),
        P(("groups", "wide"), None),
        P("wide", None),
        P("wide", None, None),
        P("wide", None, None),
        P("wide", None, None),
        P(("groups", "wide"), None),
        P(("groups", "wide"), None),
    )
    return jax.shard_map(
        body, mesh=mesh, in_specs=placed, out_specs=P(("groups", "wide"), None), check_vma=False
    )
```

time: 143 us -> 51.9 us (0.36)
  waiting for transfers between devices: 56 us -> 0 us
  Pallas kernels: 0 us -> 47.5 us
  blocking collectives: 31.2 us -> 0 us
  other arithmetic: 14 us -> 0 us
  local copies, waits for them, and re-layouts: 17 us -> 4.18 us
  matrix products: 11.6 us -> 0 us
  starting transfers between devices: 11.3 us -> 0 us
    pallas_call x0 -> x1, Pallas kernels: none -> 47.5 us  [body(): pl.pallas_call(functools.partial(layer_kernel, count), out_shape=jax.Shap...]
    ppermute x3 -> x0, waiting for transfers between devices: 33.7 us -> none  [from_partner(): return lax.ppermute(block, axis, route)]
    all_to_all x1 -> x0, blocking collectives: 31.2 us -> none  [body(): lax.all_to_all(outgoing, 'wide', split_axis=0, concat_axis=0, tiled=True)]
    all_to_all x1 -> x0, waiting for transfers between devices: 22.4 us -> none  [body(): lax.all_to_all(expert_rows(received, w_gate, w_up, w_down), 'wide', split...]
    dot_general x10 -> x0, matrix products: 11.6 us -> none  [the longest x1 4.47 us: expert_rows(): jnp.dot(activated, w_down[0], preferred_element_type=jnp.float32)]
    ppermute x3 -> x0, starting transfers between devices: 6.19 us -> none  [from_partner(): return lax.ppermute(block, axis, route)]
    gather x4 -> x0, local copies, waits for them, and re-layouts: 5.77 us -> none  [the longest x2 4.08 us: body(): hidden[source_row]]
    reshape x3 -> x0, local copies, waits for them, and re-layouts: 5.31 us -> none  [the longest x1 2.2 us: expert_rows(): return produced.reshape(received.shape)]
  transfers between devices with their start and end apart: 4 -> 0, of which waited for: 4 -> 0; matrix products, arithmetic and copies ran while one was open for 1% -> 0% of each run, Pallas kernels for 0% -> 0%
where the time goes in v1:
time: 51.9 us; the launch traced here: 51.6 us
  Pallas kernels  47.5 us (92%)
  local copies, waits for them, and re-layouts  4.18 us (8%)
    pallas_call x1, Pallas kernels, body(): pl.pallas_call(functools.partial(layer_kernel, count), out_shape=jax.Shap...  47.5 us
    unnamed x3, local copies, waits for them, and re-layouts  4.18 us

profile of v1, /device:TPU:0, one launch (start us, length us, event | category | flops | bytes accessed | tf_op | source)
XLA Modules:
  0.0 51.6 jit_solution(3233776269579995160)
XLA Ops:
  0.0 1.4 %copy.13.expert_ids = s32[16,8]{1,0:T(8,128)} copy(s32[16,8]{0,1:T(8,128)} %param.22) | data formatting | bytes 1024 | tf_op args[10]
  1.4 1.3 %copy.14.gate_weights = f32[16,8]{1,0:T(8,128)} copy(f32[16,8]{0,1:T(8,128)} %param.23) | data formatting | bytes 1024 | tf_op args[11]
  2.7 47.5 %shard_map.118 = bf16[16,2048]{1,0:T(8,128)(2,1)} custom-call(s32[4,4]{1,0:T(4,128)} %block_table.1, s32[1,4]{1,0:T(1,128)} %cache_lengths.1, bf16[128,512]{1,0:T(8,128)(2,1)} %queries_in.1, bf16[2,128,128]{2,1,0:T(8,128)(2,1)} %tree_in.1, bf16[2,16,32,128]{3,2,1,0:T(8,128)(2,1)} %cache_in.1, s32[4,32]{1,0:T(4,128)} %parents.1, bf16[512,2048]{1,0:T(8,128)(2,1)} %w_out_in.1, ...), custom_call_target="tpu_custom_call" | custom-call | tf_op jit(solution)/shard_map/pallas_call | solution.py:423
  50.2 1.5 %copy.16 = bf16[16,2048]{1,0:T(8,128)(2,1)} copy(bf16[16,2048]{1,0:T(8,128)(2,1)} %shard_map.118) | data formatting | bytes 131072

commit v2 on v1

--- a/solution.py
+++ b/solution.py
@@ -9,23 +9,27 @@
 
 ATT_TP = 8
 CHUNKS = 4
+PERIOD = 2
 TILE = 256
 LANES = 128
 MESH = pl.DeviceIdType.MESH
 
 
-def spread(bits):
+def spread(weights):
     offsets = [0]
-    for bit in bits:
-        offsets += [offset + (1 << bit) for offset in offsets]
+    for weight in weights:
+        offsets += [offset + weight for offset in offsets]
     return offsets
 
 
-def swapped(bits, low):
-    other = list(bits)
-    if len(other) > low + 1:
-        other[low], other[low + 1] = other[low + 1], other[low]
-    return other
+def swap_low(place):
+    low, high = place // 2 % 2, place // 4 % 2
+    return place - 2 * low - 4 * high + 4 * low + 2 * high
+
+
+def swapped(bits, first, second):
+    trade = {first: second, second: first}
+    return [trade.get(bit, bit) for bit in bits]
 
 
 def layer_kernel(
@@ -97,17 +101,20 @@
         )
     ):
         copy = pltpu.make_async_copy(source, target, load_sem.at[number])
-        copy.start()
+        if number < 4:
+            copy.start()
         loads.append(copy)
 
     rows = out.shape[0]
+    ids = expert_ids[...].T
+    weights_of = gate_weights[...].T
     lane_ids = lax.broadcasted_iota(jnp.int32, (rows, routing.shape[2]), 1)
     row_weight = jnp.zeros((rows, routing.shape[2]), jnp.float32)
-    for k in range(expert_ids.shape[1]):
+    for k in range(expert_ids.shape[0]):
         row_weight += jnp.where(
-            expert_ids[:, k : k + 1] == lane_ids, gate_weights[:, k : k + 1], 0.0
-        )
-    routing[me] = row_weight
+            ids[:, k : k + 1] == lane_ids, weights_of[:, k : k + 1], 0.0
+        )
+    routing_rows = row_weight
 
     seq_count, node_count = parents.shape
     head_dim = tree.shape[2]
@@ -200,36 +207,46 @@
     spans = [slice(chunk * width, (chunk + 1) * width) for chunk in range(CHUNKS)]
 
     class Halving:
-        def __init__(self, total, out_buffer, in_buffer, send_sems, recv_sems, shift, orders):
+        def __init__(self, total, out_buffer, in_buffer, send_sems, recv_sems, weights, orders):
             self.total = total
             self.out_buffer = out_buffer
             self.in_buffer = in_buffer
             self.send_sems = send_sems
             self.recv_sems = recv_sems
-            self.shift = shift
+            self.weights = weights
             self.orders = orders
             self.steps = len(orders[0])
             self.copies = {}
+            self.extra = []
 
         def places(self, chunk, step):
-            order = self.orders[chunk % 2]
+            order = self.orders[int(chunk % PERIOD == PERIOD - 1)]
             base = 0
             for bit in order[:step]:
-                base = base + mine[bit] * (1 << (bit - self.shift))
+                base = base + mine[bit] * self.weights[bit]
             bit = order[step]
-            offsets = spread([other - self.shift for other in order[step + 1 :]])
-            weight = 1 << (bit - self.shift)
+            offsets = spread([self.weights[other] for other in order[step + 1 :]] + self.extra)
+            weight = self.weights[bit]
             kept = [base + mine[bit] * weight + offset for offset in offsets]
             sent = [base + (1 - mine[bit]) * weight + offset for offset in offsets]
-            first = sum(1 << (self.steps - 1 - past) for past in range(step))
+            first = sum(
+                (1 << (self.steps - 1 - past)) << len(self.extra) for past in range(step)
+            )
             return bit, kept, sent, first
 
         def start(self, chunk, step):
+            self.fill(chunk, step)
+            self.launch(chunk, step)
+
+        def fill(self, chunk, step):
             bit, kept, sent, first = self.places(chunk, step)
             for number, place in enumerate(sent):
                 self.out_buffer[chunk, first + number] = self.total[
                     place, :, spans[chunk]
                 ].astype(jnp.bfloat16)
+
+        def launch(self, chunk, step):
+            bit, kept, sent, first = self.places(chunk, step)
             region = pl.ds(first, len(sent))
             self.copies[chunk, step] = send(
                 self.out_buffer.at[chunk, region],
@@ -248,71 +265,111 @@
                 ].astype(jnp.float32)
 
     class Doubling:
-        def __init__(self, buffer, columns, send_sems, recv_sems, row, order):
+        def __init__(self, buffer, send_sems, recv_sems, order):
             self.buffer = buffer
-            self.columns = columns
             self.send_sems = send_sems
             self.recv_sems = recv_sems
-            self.row = row
             self.order = order
             self.copies = {}
 
+        def base(self, step):
+            place = 0
+            for later in range(step, bit_count):
+                place = place + mine[self.order[later]] * (1 << later)
+            return place
+
         def start(self, step):
-            bit = self.order[step]
-            offsets = [0]
-            held = [me]
-            for past in self.order[:step]:
-                held += [place + (1 - 2 * mine[past]) * (1 << past) for place in held]
-            for number, place in enumerate(held):
-                view = self.buffer.at[place, :, self.columns]
-                slot = (1 << step) - 1 + number
-                self.copies[step, number] = send(
-                    view, view, self.send_sems.at[self.row, slot],
-                    self.recv_sems.at[self.row, slot], bit,
-                )
+            view = self.buffer.at[pl.ds(self.base(step), 1 << step)]
+            self.copies[step] = send(
+                view, view, self.send_sems.at[step], self.recv_sems.at[step], self.order[step]
+            )
 
         def finish(self, step):
-            for number in range(1 << step):
-                self.copies[step, number].wait_recv()
+            self.copies[step].wait_recv()
 
     all_bits = list(range(bit_count))
     slice_bits = all_bits[slice_shift:]
+    trade = (bit_count - 2, bit_count - 3)
+    far_bit = slice_bits[-1]
+    slice_weights = {bit: 1 << (bit - slice_shift) for bit in slice_bits}
+    place_weights = {bit: 1 << (bit_count - 1 - bit) for bit in all_bits}
     first_sum = Halving(
-        partial, send_one, recv_one, one_send_sem, one_recv_sem, slice_shift,
-        (slice_bits, swapped(slice_bits, 0)),
+        partial, send_one, recv_one, one_send_sem, one_recv_sem, slice_weights,
+        (slice_bits[:-1], swapped(slice_bits[:-1], *trade)),
     )
-    second_orders = (all_bits, swapped(all_bits, 1))
+    first_sum.extra = [slice_weights[far_bit]]
+    second_orders = (all_bits, swapped(all_bits, *trade))
     second_sum = Halving(
-        produced, send_two, recv_two, two_send_sem, two_recv_sem, 0, second_orders
+        produced, send_two, recv_two, two_send_sem, two_recv_sem, place_weights, second_orders
     )
     gathers = [
         Doubling(
-            hidden, spans[chunk], all_send_sem, all_recv_sem, chunk, second_orders[chunk % 2][::-1]
+            hidden.at[chunk], all_send_sem.at[chunk], all_recv_sem.at[chunk],
+            second_orders[int(chunk % PERIOD == PERIOD - 1)][::-1],
         )
         for chunk in range(CHUNKS)
     ]
-    route = Doubling(routing, slice(None), route_send_sem, route_recv_sem, 0, all_bits[::-1])
+    route = Doubling(routing, route_send_sem, route_recv_sem, all_bits[::-1])
+    my_place = route.base(0)
+    routing[my_place] = routing_rows
+
+    last_step = len(slice_bits) - 1
+    far_first = (1 << last_step) * 2 - 2
+
+    def far_places():
+        base = 0
+        for bit in slice_bits[:-1]:
+            base = base + mine[bit] * slice_weights[bit]
+        return [base, base + slice_weights[far_bit]]
+
+    far_copies = {}
+
+    def far_start(chunk):
+        for number, place in enumerate(far_places()):
+            send_one[chunk, far_first + number] = partial[place, :, spans[chunk]].astype(
+                jnp.bfloat16
+            )
+        region = pl.ds(far_first, 2)
+        far_copies[chunk] = send(
+            send_one.at[chunk, region], recv_one.at[chunk, region],
+            one_send_sem.at[chunk, last_step], one_recv_sem.at[chunk, last_step], far_bit,
+        )
+
+    def far_finish(chunk):
+        far_copies[chunk].wait_recv()
+        base = gathers[chunk].base(1)
+        for number, place in enumerate(far_places()):
+            hidden[chunk, base + number] = (
+                partial[place, :, spans[chunk]]
+                + recv_one[chunk, far_first + number].astype(jnp.float32)
+            ).astype(jnp.bfloat16)
 
     loads[3].wait()
-    pl.semaphore_wait(barrier, bit_count)
+    for copy in loads[4:]:
+        copy.start()
     for chunk in range(CHUNKS):
         projected = jnp.dot(
             attended[...], w_out[:, spans[chunk]], preferred_element_type=jnp.float32
         )
         partial[:, :, spans[chunk]] = projected.reshape(partial.shape[0], rows, width)
-        first_sum.start(chunk, 0)
+        first_sum.fill(chunk, 0)
+    pl.semaphore_wait(barrier, bit_count)
+    for chunk in range(CHUNKS):
+        first_sum.launch(chunk, 0)
     route.start(0)
-    for step in range(first_sum.steps):
+    for step in range(last_step):
         for chunk in range(CHUNKS):
             first_sum.finish(chunk, step)
-            if step + 1 < first_sum.steps:
+            if step + 1 < last_step:
                 first_sum.start(chunk, step + 1)
             else:
-                hidden[me, :, spans[chunk]] = partial[
-                    me // (1 << slice_shift), :, spans[chunk]
-                ].astype(jnp.bfloat16)
-                gathers[chunk].start(0)
-    for step in range(bit_count):
+                far_start(chunk)
+    route.finish(0)
+    route.start(1)
+    for chunk in range(CHUNKS):
+        far_finish(chunk)
+        gathers[chunk].start(1)
+    for step in range(1, bit_count):
         for chunk in range(CHUNKS):
             if step + 1 < bit_count:
                 gathers[chunk].finish(step)
@@ -341,9 +398,11 @@
         gathers[chunk].finish(bit_count - 1)
 
         def accumulate(group, chunk=chunk):
-            taken = hidden[pl.ds(group * blocks, blocks), :, spans[chunk]].reshape(
-                tile_rows, width
-            )
+            taken = hidden[chunk, pl.ds(group * blocks, blocks)]
+            if chunk % PERIOD == PERIOD - 1:
+                order = [swap_low(block) for block in range(blocks)]
+                taken = jnp.concatenate([taken[block : block + 1] for block in order], axis=0)
+            taken = taken.reshape(tile_rows, width)
             for cut in cuts:
                 for sums, weights in ((gate_sum, w_gate), (up_sum, w_up)):
                     part = jnp.dot(
@@ -386,7 +445,7 @@
             if step + 1 < second_sum.steps:
                 second_sum.start(chunk, step + 1)
             else:
-                out[:, spans[chunk]] = produced[me, :, spans[chunk]].astype(jnp.bfloat16)
+                out[:, spans[chunk]] = produced[my_place, :, spans[chunk]].astype(jnp.bfloat16)
     for copy in started:
         copy.wait_send()
 
@@ -435,23 +494,23 @@
             pltpu.VMEM(w_down.shape[1:], w_down.dtype),
             pltpu.VMEM(queries.shape, jnp.bfloat16),
             pltpu.VMEM((ATT_TP, rows, features), jnp.float32),
-            pltpu.VMEM((count, rows, features), jnp.bfloat16),
+            pltpu.VMEM((CHUNKS, count, rows, width), jnp.bfloat16),
             pltpu.VMEM((count, rows, lanes), jnp.float32),
             pltpu.VMEM((groups, tile_rows, hidden_width), jnp.float32),
             pltpu.VMEM((groups, tile_rows, hidden_width), jnp.float32),
             pltpu.VMEM((groups, tile_rows, hidden_width), jnp.bfloat16),
             pltpu.VMEM((count, rows, features), jnp.float32),
-            pltpu.VMEM((CHUNKS, ATT_TP - 1, rows, width), jnp.bfloat16),
-            pltpu.VMEM((CHUNKS, ATT_TP - 1, rows, width), jnp.bfloat16),
+            pltpu.VMEM((CHUNKS, ATT_TP, rows, width), jnp.bfloat16),
+            pltpu.VMEM((CHUNKS, ATT_TP, rows, width), jnp.bfloat16),
             pltpu.VMEM((CHUNKS, count - 1, rows, width), jnp.bfloat16),
             pltpu.VMEM((CHUNKS, count - 1, rows, width), jnp.bfloat16),
             dma((7,)),
             dma((CHUNKS, slice_steps)),
             dma((CHUNKS, slice_steps)),
-            dma((CHUNKS, count - 1)),
-            dma((CHUNKS, count - 1)),
-            dma((1, count - 1)),
-            dma((1, count - 1)),
+            dma((CHUNKS, bit_count)),
+            dma((CHUNKS, bit_count)),
+            dma((bit_count,)),
+            dma((bit_count,)),
             dma((CHUNKS, bit_count)),
             dma((CHUNKS, bit_count)),
         ],
@@ -469,8 +528,8 @@
         w_gate,
         w_up,
         w_down,
-        expert_ids,
-        gate_weights,
+        expert_ids.T,
+        gate_weights.T,
     )
 
 

time: 51.9 us -> 44.4 us (0.86)
  Pallas kernels: 47.5 us -> 42.7 us
  local copies, waits for them, and re-layouts: 4.18 us -> 1.47 us
    pallas_call x1, Pallas kernels: 47.5 us -> 42.7 us  [body(): pl.pallas_call(functools.partial(layer_kernel, count), out_shape=jax.Shap...]
    unnamed x3 -> x1, local copies, waits for them, and re-layouts: 4.18 us -> 1.47 us
where the time goes in v2:
time: 44.4 us; the launch traced here: 44.2 us
  Pallas kernels  42.7 us (96%)
  local copies, waits for them, and re-layouts  1.47 us (3%)
    pallas_call x1, Pallas kernels, body(): pl.pallas_call(functools.partial(layer_kernel, count), out_shape=jax.Shap...  42.7 us
    unnamed x1, local copies, waits for them, and re-layouts  1.47 us

profile of v2, /device:TPU:0, one launch (start us, length us, event | category | flops | bytes accessed | tf_op | source)
XLA Modules:
  0.0 44.2 jit_solution(8181281167751010896)
XLA Ops:
  0.0 42.7 %shard_map.118 = bf16[16,2048]{1,0:T(8,128)(2,1)} custom-call(s32[4,4]{1,0:T(4,128)} %block_table.1, s32[1,4]{1,0:T(1,128)} %cache_lengths.1, bf16[128,512]{1,0:T(8,128)(2,1)} %queries_in.1, bf16[2,128,128]{2,1,0:T(8,128)(2,1)} %tree_in.1, bf16[2,16,32,128]{3,2,1,0:T(8,128)(2,1)} %cache_in.1, s32[4,32]{1,0:T(4,128)} %parents.1, bf16[512,2048]{1,0:T(8,128)(2,1)} %w_out_in.1, ...), custom_call_target="tpu_custom_call" | custom-call | tf_op jit(solution)/shard_map/pallas_call | solution.py:482
  42.7 1.5 %copy.14 = bf16[16,2048]{1,0:T(8,128)(2,1)} copy(bf16[16,2048]{1,0:T(8,128)(2,1)} %shard_map.118) | data formatting | bytes 131072
